TPU v7x, 256 devices: a whole 4x4x8 slice. The times are simulated.
256 devices in a mesh: cfg: 2 (over x_lo), wide: 32 (over x_hi, z, core), narrow: 4 (over y).
Axes of the slice: x: 4 (x_hi: 2, x_lo: 2; x = x_hi * 2 + x_lo), y: 4, z: 8, core: 2. Of those that a mesh axis runs over, the one named last changes fastest.
Arguments:
- hidden: bfloat16 [2, 4096, 3072], P('cfg', 'wide', 'narrow'), may hold values from -120 to 120
- split_table: int32 [32], replicated, may hold values from 1 to 128, 2048 in all
- modulation: float32 [8, 3072], P(None, 'narrow'), may hold values from -4 to 4
- expand_weight: bfloat16 [3072, 12288], P('narrow', 'wide'), may hold values from -0.109375 to 0.109375
- contract_weight: bfloat16 [12288, 3072], P('wide', 'narrow'), may hold values from -0.0546875 to 0.0546875
- output_weight: bfloat16 [3072, 64], P('narrow'), may hold values from -0.109375 to 0.109375
- latent: float32 [4096, 64], P('wide'), may hold values from -6 to 6
- timestep: int32 [1], replicated, may hold values from 20 to 499
Outputs:
- layer_out: bfloat16 [2, 4096, 3072], P('cfg', 'wide', 'narrow')
- clean_latent: float32 [4096, 64], P('wide')
Inputs may be any that keep to these rules, and one draw needn't show every extreme that they name: `split_table`: the entries sum to 2048, and the largest is exactly 128.
All inputs are finite; a program needn't handle non-finite values.
Results may differ from a plain program's by a relative error of at most 0.0056.
Values may be sent and summed in bfloat16 or wider, within the bound.
A program may use at most 64 MiB of HBM per device.

v0:
```python
import jax
import jax.numpy as jnp
from jax import lax
from jax.sharding import PartitionSpec as P

D = 3072
TEXT = 226
norm_eps = 1e-05
guidance = 6.0


def alpha_table():
    steps_index = jnp.arange(1000, dtype=jnp.int32)
    start_root = 0.00085**0.5
    end_root = 0.012**0.5
    roots = start_root + (end_root - start_root) * steps_index.astype(jnp.float32) / 999.0
    return (steps_index, jnp.cumprod(1.0 - roots * roots))


def feature_norm(values, shifts, scaling):
    totals, squares = lax.psum(
        (jnp.sum(values, -1, keepdims=True), jnp.sum(values * values, -1, keepdims=True)), "narrow"
    )
    average = totals / D
    variance = squares / D - average * average
    return (values - average) * lax.rsqrt(variance + norm_eps) * (1.0 + scaling) + shifts


def on_device(
    hidden, split_table, modulation, expand_weight, contract_weight, output_weight, latent, timestep
):
    capacity = hidden.shape[1]
    wide_index = lax.axis_index("wide")
    table_index = jnp.arange(split_table.shape[0], dtype=jnp.int32)
    offset = jnp.sum(jnp.where(table_index < wide_index, split_table, 0))
    own_count = jnp.sum(jnp.where(table_index == wide_index, split_table, 0))
    slot_index = jnp.arange(capacity, dtype=jnp.int32)
    position = offset + slot_index
    slot_live = slot_index < own_count
    is_text = slot_live & (position < TEXT)
    is_video = slot_live & (position >= TEXT)
    text_column = is_text[:, None]
    shifts = jnp.where(text_column, modulation[3], modulation[0])
    scaling = jnp.where(text_column, modulation[4], modulation[1])
    gating = jnp.where(text_column, modulation[5], modulation[2])
    values = hidden[0].astype(jnp.float32)
    normed = feature_norm(values, shifts, scaling).astype(jnp.bfloat16)
    hidden_part = jnp.dot(
        lax.all_gather(normed, "wide", axis=0, tiled=True),
        expand_weight,
        preferred_element_type=jnp.float32,
    )
    hidden_pre = lax.psum(hidden_part, "narrow")
    activated = jax.nn.gelu(hidden_pre, approximate=True).astype(jnp.bfloat16)
    ff_result = lax.psum_scatter(
        jnp.dot(activated, contract_weight, preferred_element_type=jnp.float32),
        "wide",
        scatter_dimension=0,
        tiled=True,
    )
    layer_out = jnp.where(slot_live[:, None], values + gating * ff_result, 0.0).astype(jnp.bfloat16)
    final_in = layer_out.astype(jnp.float32)
    final_normed = feature_norm(final_in, modulation[6], modulation[7]).astype(jnp.bfloat16)
    velocity_part = jnp.dot(final_normed, output_weight, preferred_element_type=jnp.float32)
    copy_weight = jnp.where(lax.axis_index("cfg") == 0, guidance, 1.0 - guidance)
    guided = lax.psum(velocity_part * copy_weight, ("cfg", "narrow"))
    steps_index, alpha_bar = alpha_table()
    alpha_now = jnp.sum(jnp.where(steps_index == timestep[0], alpha_bar, 0.0))
    clean_latent = jnp.where(
        is_video[:, None], jnp.sqrt(alpha_now) * latent - jnp.sqrt(1.0 - alpha_now) * guided, 0.0
    )
    return (layer_out[None], clean_latent)


def solution(mesh):
    return jax.shard_map(
        on_device,
        mesh=mesh,
        in_specs=(
            P("cfg", "wide", "narrow"),
            P(),
            P(None, "narrow"),
            P("narrow", "wide"),
            P("wide", "narrow"),
            P("narrow", None),
            P("wide", None),
            P(),
        ),
        out_specs=(P("cfg", "wide", "narrow"), P("wide", None)),
        check_vma=False,
    )
```

profile of v0, /device:TPU:2, one launch (start us, length us, event | category | flops | bytes accessed | tf_op | source)
XLA Modules:
  0.0 493.6 jit_solution(13559903819700724804)
XLA Ops:
  7.2 0.0 copy-start
  7.2 0.0 all-gather.2.cloned.1.call-start
  7.2 1.1 convert_reduce_fusion.1
  8.3 1.1 fusion.21
  9.4 1.1 add_reduce_fusion
  10.5 1.3 fusion.34
  11.8 1.3 compare_and_fusion.1
  13.1 10.7 %all-reduce.2 = (f32[128,1]{0,1:T(1,128)S(1)}, f32[128,1]{0,1:T(1,128)S(1)}) all-reduce(f32[128,1]{0,1:T(1,128)S(1)} %bitcast.48, f32[128,1]{0,1:T(1,128)S(1)} %bitcast.47), channel_id=1, replica_groups=mesh['cfg'=2,'wide'=32,'narrow'=4] {'narrow'}, use_global_device_ids=true, to_apply=%region_5.6 | all-reduce | flops 256 | bytes 2048 | tf_op jit(solution)/shard_map/psum | solution.py:21
  23.8 1.8 fusion.20
  25.7 0.0 all-gather.2.cloned.1.call-update
  25.7 0.0 all-reduce.5.cloned.1.call-start
  25.7 94.3 %all-gather.2.cloned.1.call-done = bf16[4096,768]{1,0:T(8,128)(2,1)} async-done(((bf16[128,768]{1,0:T(8,128)(2,1)}), bf16[4096,768]{1,0:T(8,128)(2,1)}) %all-gather.2.cloned.1.call-update) | async-done | bytes 6291472 | tf_op jit(solution)/shard_map/all_gather | solution.py:49
  120.1 9.0 %fusion.41 = f32[4096,384]{1,0:T(8,128)} fusion(bf16[4096,768]{1,0:T(8,128)(2,1)} %all-gather.2.cloned.1.call-done, bf16[768,384]{1,0:T(8,128)(2,1)} %param.11), kind=kOutput, calls=%fused_computation.70 | convolution fusion | flops 2415919104 | bytes 13172736 | tf_op jit(solution)/shard_map/dot_general | solution.py:48
  129.0 0.0 all-reduce.5.cloned.1.call-update
  129.1 0.0 reduce-scatter.2.cloned.1.call-start
  129.1 129.7 %all-reduce.5.cloned.1.call-done = f32[4096,384]{1,0:T(8,128)} async-done(((f32[4096,384]{1,0:T(8,128)}), f32[4096,384]{1,0:T(8,128)}) %all-reduce.5.cloned.1.call-update) | async-done | bytes 6291472 | tf_op jit(solution)/shard_map/psum | solution.py:53
  258.8 11.8 %fusion.8 = f32[4096,768]{1,0:T(8,128)} fusion(bf16[384,768]{1,0:T(8,128)(2,1)S(1)} %copy-done, f32[4096,384]{1,0:T(8,128)} %all-reduce.5.cloned.1.call-done), kind=kOutput, calls=%fused_computation.9 | convolution fusion | flops 2430074880 | bytes 19464192 | tf_op jit(solution)/shard_map/dot_general | solution.py:56
  270.6 0.0 reduce-scatter.2.cloned.1.call-update
  270.7 0.3 reduce-window.9
  271.0 0.1 slice.40
  271.7 0.1 slice_reduce_fusion
  271.8 0.1 multiply_bitcast_fusion
  271.9 0.7 select_reduce_fusion
  274.0 0.7 iota_compare_fusion.1
  274.7 1.3 compare_and_fusion
  275.9 167.3 %reduce-scatter.2.cloned.1.call-done = f32[128,768]{1,0:T(8,128)} async-done(((f32[4096,768]{1,0:T(8,128)}), f32[128,768]{1,0:T(8,128)}) %reduce-scatter.2.cloned.1.call-update) | async-done | bytes 393232 | tf_op jit(solution)/shard_map/reduce_scatter | solution.py:55
  443.2 1.3 convert_reduce_fusion
  444.5 0.0 copy-start.2
  444.5 10.5 %all-reduce.1 = (f32[128,1]{0,1:T(1,128)S(1)}, f32[128,1]{0,1:T(1,128)S(1)}) all-reduce(f32[128,1]{0,1:T(1,128)S(1)} %bitcast.50, f32[128,1]{0,1:T(1,128)S(1)} %bitcast.49), channel_id=1, replica_groups=mesh['cfg'=2,'wide'=32,'narrow'=4] {'narrow'}, use_global_device_ids=true, to_apply=%region_14.15 | all-reduce | flops 256 | bytes 2048 | tf_op jit(solution)/shard_map/psum | solution.py:21
  455.0 0.3 convolution_multiply_fusion
  455.3 31.1 %psum.47 = f32[128,64]{0,1:T(8,128)S(1)} all-reduce(f32[128,64]{0,1:T(8,128)S(1)} %convolution_multiply_fusion), channel_id=1, replica_groups=mesh['cfg'=2,'wide'=32,'narrow'=4] {'cfg','narrow'}, use_global_device_ids=true, to_apply=%region_15.16 | all-reduce | flops 8192 | bytes 65536 | tf_op jit(solution)/shard_map/psum | solution.py:66
  486.4 0.6 subtract_select_fusion
  (13 shorter events, 0.1 us)
Async XLA Ops:
  7.2 251.7 %copy-start = (bf16[384,768]{1,0:T(8,128)(2,1)S(1)}, bf16[384,768]{1,0:T(8,128)(2,1)}, u32[]{:S(2)}) copy-start(bf16[384,768]{1,0:T(8,128)(2,1)} %param.12) | copy-start | bytes 1769476
  7.2 112.9 %all-gather.2.cloned.1.call-start = ((), (), s32[]{:S(2)}) async-start(), calls=%async_computation.1 | async-start | bytes 6488064 | tf_op jit(solution)/shard_map/all_gather | solution.py:49
  25.7 233.1 %all-reduce.5.cloned.1.call-start = ((), (), s32[]{:S(2)}) async-start(), calls=%async_computation.2 | async-start | bytes 12582912 | tf_op jit(solution)/shard_map/psum | solution.py:53
  129.1 314.2 %reduce-scatter.2.cloned.1.call-start = ((), (), s32[]{:S(2)}) async-start(), calls=%async_computation.3 | async-start | bytes 12976128 | tf_op jit(solution)/shard_map/reduce_scatter | solution.py:55
  270.6 172.6 %copy-start.1 = (bf16[1,128,768]{2,1,0:T(8,128)(2,1)S(1)}, bf16[1,128,768]{2,1,0:T(8,128)(2,1)}, u32[]{:S(2)}) copy-start(bf16[1,128,768]{2,1,0:T(8,128)(2,1)} %param.8) | copy-start | bytes 589828
  270.6 184.4 %copy-start.4 = (bf16[768,64]{0,1:T(8,128)(2,1)S(1)}, bf16[768,64]{0,1:T(8,128)(2,1)}, u32[]{:S(2)}) copy-start(bf16[768,64]{0,1:T(8,128)(2,1)} %param.13) | copy-start | bytes 294916
  270.6 215.8 %copy-start.3 = (f32[128,64]{0,1:T(8,128)S(1)}, f32[128,64]{0,1:T(8,128)}, u32[]{:S(2)}) copy-start(f32[128,64]{0,1:T(8,128)} %param.14) | copy-start | bytes 98308
  444.5 42.6 %copy-start.2 = (bf16[128,768]{1,0:T(8,128)(2,1)}, bf16[128,768]{1,0:T(8,128)(2,1)S(1)}, u32[]{:S(2)}) copy-start(bf16[128,768]{1,0:T(8,128)(2,1)S(1)} %get-tuple-element.18) | copy-start | bytes 589828
Sparse Core Ops, SparseCore 0:
  25.8 94.2 all-gather.1
  129.2 129.5 all-reduce.4
  270.8 172.3 reduce-scatter.1
where the time goes:
time: 494 us
  waiting for transfers between devices  391 us (79%)
  blocking collectives  52.4 us (11%)
  matrix products  21.1 us (4%)
  between operations  15.9 us (3%)
  other arithmetic  12.5 us (3%)
    reduce_scatter x1, waiting for transfers between devices, on_device(): lax.psum_scatter(jnp.dot(activated, contract_weight, preferred_element_ty...  167 us
    psum x1, waiting for transfers between devices, on_device(): hidden_pre = lax.psum(hidden_part, 'narrow')  130 us
    all_gather x1, waiting for transfers between devices, on_device(): lax.all_gather(normed, 'wide', axis=0, tiled=True)  94.3 us
    psum x1, blocking collectives, on_device(): guided = lax.psum(velocity_part * copy_weight, ('cfg', 'narrow'))  31.1 us
    psum x2, blocking collectives, feature_norm(): lax.psum((jnp.sum(values, -1, keepdims=True), jnp.sum(values * values, -1...  21.2 us
    dot_general x1, matrix products, on_device(): jnp.dot(activated, contract_weight, preferred_element_type=jnp.float32)  11.8 us
  transfers between devices with their start and end apart: 3, of which 3 were waited for; matrix products, arithmetic and copies ran while one was open for 1% of the time, Pallas kernels for 0%

commit v1 on v0

--- a/solution.py
+++ b/solution.py
@@ -50,7 +50,11 @@
         expand_weight,
         preferred_element_type=jnp.float32,
     )
-    hidden_pre = lax.psum(hidden_part, "narrow")
+    hidden_pre = hidden_part
+    for hop in (1, 2):
+        hidden_pre = hidden_pre + lax.ppermute(
+            hidden_pre, "narrow", [(dev, dev ^ hop) for dev in range(4)]
+        )
     activated = jax.nn.gelu(hidden_pre, approximate=True).astype(jnp.bfloat16)
     ff_result = lax.psum_scatter(
         jnp.dot(activated, contract_weight, preferred_element_type=jnp.float32),

time: 494 us -> 635 us (1.29)
  waiting for transfers between devices: 391 us -> 531 us
  matrix products: 21.1 us -> 13.5 us
    ppermute x0 -> x2, waiting for transfers between devices: none -> 272 us  [on_device(): lax.ppermute(hidden_pre, 'narrow', [(dev, dev ^ hop) for dev in range(4)])]
    psum x1 -> x0, waiting for transfers between devices: 130 us -> none  [on_device(): hidden_pre = lax.psum(hidden_part, 'narrow')]
  transfers between devices with their start and end apart: 3 -> 4, of which waited for: 3 -> 4; matrix products, arithmetic and copies ran while one was open for 1% -> 1% of each run, Pallas kernels for 0% -> 0%
where the time goes in v1:
time: 635 us; the launch traced here: 634 us
  waiting for transfers between devices  531 us (84%)
  blocking collectives  52.4 us (8%)
  between operations  16.1 us (3%)
  other arithmetic  16 us (3%)
  matrix products  13.5 us (2%)
    ppermute x2, waiting for transfers between devices, on_device(): lax.ppermute(hidden_pre, 'narrow', [(dev, dev ^ hop) for dev in range(4)])  272 us
    reduce_scatter x1, waiting for transfers between devices, on_device(): lax.psum_scatter(jnp.dot(activated, contract_weight, preferred_element_ty...  165 us
    all_gather x1, waiting for transfers between devices, on_device(): lax.all_gather(normed, 'wide', axis=0, tiled=True)  94.3 us
    psum x1, blocking collectives, on_device(): guided = lax.psum(velocity_part * copy_weight, ('cfg', 'narrow'))  31.2 us
    psum x2, blocking collectives, feature_norm(): lax.psum((jnp.sum(values, -1, keepdims=True), jnp.sum(values * values, -1...  21.2 us
  transfers between devices with their start and end apart: 4, of which 4 were waited for; matrix products, arithmetic and copies ran while one was open for 1% of the time, Pallas kernels for 0%

profile of v1, /device:TPU:2, one launch (start us, length us, event | category | flops | bytes accessed | tf_op | source)
XLA Modules:
  0.0 634.2 jit_solution(18267271048913999860)
XLA Ops:
  7.2 0.0 all-gather.2.cloned.1.call-start
  7.2 1.1 convert_reduce_fusion.1
  8.3 1.1 fusion.21
  9.4 1.1 add_reduce_fusion
  10.5 1.4 fusion.34
  11.8 1.3 compare_and_fusion.1
  13.2 10.7 %all-reduce.2 = (f32[128,1]{0,1:T(1,128)S(1)}, f32[128,1]{0,1:T(1,128)S(1)}) all-reduce(f32[128,1]{0,1:T(1,128)S(1)} %bitcast.48, f32[128,1]{0,1:T(1,128)S(1)} %bitcast.47), channel_id=1, replica_groups=mesh['cfg'=2,'wide'=32,'narrow'=4] {'narrow'}, use_global_device_ids=true, to_apply=%region_5.6 | all-reduce | flops 256 | bytes 2048 | tf_op jit(solution)/shard_map/psum | solution.py:21
  23.9 1.8 fusion.20
  25.8 0.0 all-gather.2.cloned.1.call-update
  25.8 0.0 reduce-scatter.2.cloned.1.call-start
  25.8 94.3 %all-gather.2.cloned.1.call-done = bf16[4096,768]{1,0:T(8,128)(2,1)} async-done(((bf16[128,768]{1,0:T(8,128)(2,1)}), bf16[4096,768]{1,0:T(8,128)(2,1)}) %all-gather.2.cloned.1.call-update) | async-done | bytes 6291472 | tf_op jit(solution)/shard_map/all_gather | solution.py:49
  120.2 5.6 fusion.41
  125.8 1.6 collective-permute-start
  127.4 136.3 %collective-permute-done = f32[4096,384]{1,0:T(8,128)} collective-permute-done((f32[4096,384]{1,0:T(8,128)S(1)}, f32[4096,384]{1,0:T(8,128)}, u32[]{:S(2)}, u32[]{:S(2)}) %collective-permute-start) | collective-permute-done | bytes 6291488 | tf_op jit(solution)/shard_map/ppermute | solution.py:55
  263.7 3.4 add.89
  267.1 3.1 collective-permute-start.1
  270.2 135.4 %collective-permute-done.1 = f32[4096,384]{1,0:T(8,128)S(1)} collective-permute-done((f32[4096,384]{1,0:T(8,128)S(1)}, f32[4096,384]{1,0:T(8,128)S(1)}, u32[]{:S(2)}, u32[]{:S(2)}) %collective-permute-start.1) | collective-permute-done | bytes 6291488 | tf_op jit(solution)/shard_map/ppermute | solution.py:55
  405.5 7.6 %fusion.8 = f32[4096,768]{1,0:T(8,128)} fusion(bf16[384,768]{1,0:T(8,128)(2,1)S(1)} %copy-done, f32[4096,384]{1,0:T(8,128)S(1)} %add.89, f32[4096,384]{1,0:T(8,128)S(1)} %collective-permute-done.1), kind=kOutput, calls=%fused_computation.9 | convolution fusion | flops 2431647744 | bytes 25755648 | tf_op jit(solution)/shard_map/dot_general | solution.py:60
  413.1 0.0 reduce-scatter.2.cloned.1.call-update
  413.2 0.3 reduce-window.9
  413.4 0.1 slice.40
  414.2 0.1 slice_reduce_fusion
  414.3 0.1 multiply_bitcast_fusion
  414.4 0.6 select_reduce_fusion
  416.3 0.7 iota_compare_fusion.1
  417.0 1.3 compare_and_fusion
  418.3 165.1 %reduce-scatter.2.cloned.1.call-done = f32[128,768]{1,0:T(8,128)} async-done(((f32[4096,768]{1,0:T(8,128)}), f32[128,768]{1,0:T(8,128)}) %reduce-scatter.2.cloned.1.call-update) | async-done | bytes 393232 | tf_op jit(solution)/shard_map/reduce_scatter | solution.py:59
  583.4 1.3 convert_reduce_fusion
  584.7 10.5 %all-reduce.1 = (f32[128,1]{0,1:T(1,128)S(1)}, f32[128,1]{0,1:T(1,128)S(1)}) all-reduce(f32[128,1]{0,1:T(1,128)S(1)} %bitcast.50, f32[128,1]{0,1:T(1,128)S(1)} %bitcast.49), channel_id=1, replica_groups=mesh['cfg'=2,'wide'=32,'narrow'=4] {'narrow'}, use_global_device_ids=true, to_apply=%region_13.14 | all-reduce | flops 256 | bytes 2048 | tf_op jit(solution)/shard_map/psum | solution.py:21
  595.2 0.3 convolution_multiply_fusion
  595.5 31.2 %psum.39 = f32[128,64]{0,1:T(8,128)S(1)} all-reduce(f32[128,64]{0,1:T(8,128)S(1)} %convolution_multiply_fusion), channel_id=1, replica_groups=mesh['cfg'=2,'wide'=32,'narrow'=4] {'cfg','narrow'}, use_global_device_ids=true, to_apply=%region_14.15 | all-reduce | flops 8192 | bytes 65536 | tf_op jit(solution)/shard_map/psum | solution.py:70
  626.7 0.6 subtract_select_fusion
  (15 shorter events, 0.1 us)
Async XLA Ops:
  7.2 398.4 %copy-start = (bf16[384,768]{1,0:T(8,128)(2,1)S(1)}, bf16[384,768]{1,0:T(8,128)(2,1)}, u32[]{:S(2)}) copy-start(bf16[384,768]{1,0:T(8,128)(2,1)} %param.12) | copy-start | bytes 1769476
  7.2 113.0 %all-gather.2.cloned.1.call-start = ((), (), s32[]{:S(2)}) async-start(), calls=%async_computation.1 | async-start | bytes 6488064 | tf_op jit(solution)/shard_map/all_gather | solution.py:49
  25.8 557.7 %reduce-scatter.2.cloned.1.call-start = ((), (), s32[]{:S(2)}) async-start(), calls=%async_computation.2 | async-start | bytes 12976128 | tf_op jit(solution)/shard_map/reduce_scatter | solution.py:59
  125.8 137.9 %collective-permute-start = (f32[4096,384]{1,0:T(8,128)S(1)}, f32[4096,384]{1,0:T(8,128)}, u32[]{:S(2)}, u32[]{:S(2)}) collective-permute-start(f32[4096,384]{1,0:T(8,128)S(1)} %fusion.41), channel_id=1, source_target_pairs={{0,1},{1,0},{2,3},{3,2},{4,5},{5,4},{6,7},{7,6},{8,9},{9,8},{10,11... | collective-permute-start | bytes 18874376 | tf_op jit(solution)/shard_map/ppermute | solution.py:55
  267.1 138.5 %collective-permute-start.1 = (f32[4096,384]{1,0:T(8,128)S(1)}, f32[4096,384]{1,0:T(8,128)S(1)}, u32[]{:S(2)}, u32[]{:S(2)}) collective-permute-start(f32[4096,384]{1,0:T(8,128)S(1)} %add.89), channel_id=1, source_target_pairs={{0,2},{1,3},{2,0},{3,1},{4,6},{5,7},{6,4},{7,5},{8,10},{9,11},{10,... | collective-permute-start | bytes 18874376 | tf_op jit(solution)/shard_map/ppermute | solution.py:55
  413.1 170.3 %copy-start.1 = (bf16[1,128,768]{2,1,0:T(8,128)(2,1)S(1)}, bf16[1,128,768]{2,1,0:T(8,128)(2,1)}, u32[]{:S(2)}) copy-start(bf16[1,128,768]{2,1,0:T(8,128)(2,1)} %param.8) | copy-start | bytes 589828
  413.1 182.1 %copy-start.4 = (bf16[768,64]{0,1:T(8,128)(2,1)S(1)}, bf16[768,64]{0,1:T(8,128)(2,1)}, u32[]{:S(2)}) copy-start(bf16[768,64]{0,1:T(8,128)(2,1)} %param.13) | copy-start | bytes 294916
  413.1 213.6 %copy-start.3 = (f32[128,64]{0,1:T(8,128)S(1)}, f32[128,64]{0,1:T(8,128)}, u32[]{:S(2)}) copy-start(f32[128,64]{0,1:T(8,128)} %param.14) | copy-start | bytes 98308
  584.7 42.6 %copy-start.2 = (bf16[128,768]{1,0:T(8,128)(2,1)}, bf16[128,768]{1,0:T(8,128)(2,1)S(1)}, u32[]{:S(2)}) copy-start(bf16[128,768]{1,0:T(8,128)(2,1)S(1)} %get-tuple-element.18) | copy-start | bytes 589828
Sparse Core Ops, SparseCore 0:
  25.9 94.2 all-gather.1
  413.3 170.1 reduce-scatter.1

commit v2 on v0

--- a/solution.py
+++ b/solution.py
@@ -46,7 +46,9 @@
     values = hidden[0].astype(jnp.float32)
     normed = feature_norm(values, shifts, scaling).astype(jnp.bfloat16)
     hidden_part = jnp.dot(
-        lax.all_gather(normed, "wide", axis=0, tiled=True),
+        jnp.concatenate(
+            lax.all_to_all(jnp.stack([normed] * lax.axis_size("wide")), "wide", 0, 0), axis=0
+        ),
         expand_weight,
         preferred_element_type=jnp.float32,
     )

time: 494 us -> 546 us (1.11)
  blocking collectives: 52.4 us -> 205 us
  waiting for transfers between devices: 391 us -> 294 us
    all_to_all x0 -> x1, blocking collectives: none -> 153 us  [on_device(): lax.all_to_all(jnp.stack([normed] * lax.axis_size('wide')), 'wide', 0, 0)]
    all_gather x1 -> x0, waiting for transfers between devices: 94.3 us -> none  [on_device(): lax.all_gather(normed, 'wide', axis=0, tiled=True)]
  transfers between devices with their start and end apart: 3 -> 2, of which waited for: 3 -> 2; matrix products, arithmetic and copies ran while one was open for 1% -> 1% of each run, Pallas kernels for 0% -> 0%
where the time goes in v2:
time: 546 us; the launch traced here: 545 us
  waiting for transfers between devices  294 us (54%)
  blocking collectives  205 us (38%)
  matrix products  17.4 us (3%)
  between operations  16.1 us (3%)
  other arithmetic  11.8 us (2%)
    reduce_scatter x1, waiting for transfers between devices, on_device(): lax.psum_scatter(jnp.dot(activated, contract_weight, preferred_element_ty...  167 us
    all_to_all x1, blocking collectives, on_device(): lax.all_to_all(jnp.stack([normed] * lax.axis_size('wide')), 'wide', 0, 0)  153 us
    psum x1, waiting for transfers between devices, on_device(): hidden_pre = lax.psum(hidden_part, 'narrow')  126 us
    psum x1, blocking collectives, on_device(): guided = lax.psum(velocity_part * copy_weight, ('cfg', 'narrow'))  31.1 us
    psum x2, blocking collectives, feature_norm(): lax.psum((jnp.sum(values, -1, keepdims=True), jnp.sum(values * values, -1...  21.2 us
    dot_general x1, matrix products, on_device(): jnp.dot(activated, contract_weight, preferred_element_type=jnp.float32)  11.8 us
  transfers between devices with their start and end apart: 2, of which 2 were waited for; matrix products, arithmetic and copies ran while one was open for 1% of the time, Pallas kernels for 0%

profile of v2, /device:TPU:2, one launch (start us, length us, event | category | flops | bytes accessed | tf_op | source)
XLA Modules:
  0.0 545.2 jit_solution(15397178398979958435)
XLA Ops:
  7.2 0.0 copy-start
  7.2 0.0 all-reduce.5.cloned.1.call-start
  7.2 1.1 convert_reduce_fusion.1
  8.3 1.1 fusion.16
  9.4 1.1 add_reduce_fusion
  10.5 1.3 fusion.34
  11.8 1.3 compare_and_fusion.1
  13.1 10.7 %all-reduce.2 = (f32[128,1]{0,1:T(1,128)S(1)}, f32[128,1]{0,1:T(1,128)S(1)}) all-reduce(f32[128,1]{0,1:T(1,128)S(1)} %bitcast.42, f32[128,1]{0,1:T(1,128)S(1)} %bitcast.41), channel_id=1, replica_groups=mesh['cfg'=2,'wide'=32,'narrow'=4] {'narrow'}, use_global_device_ids=true, to_apply=%region_5.6 | all-reduce | flops 256 | bytes 2048 | tf_op jit(solution)/shard_map/psum | solution.py:21
  23.8 1.1 fusion.29
  25.0 0.7 stack.5
  25.7 0.0 copy-start.4
  25.7 152.6 %all_to_all.5 = bf16[32,128,768]{2,1,0:T(8,128)(2,1)S(1)} all-to-all(bf16[32,128,768]{2,1,0:T(8,128)(2,1)S(1)} %stack.5), channel_id=1, replica_groups=mesh['cfg'=2,'wide'=32,'narrow'=4] {'wide'}, dimensions={0} | all-to-all | bytes 12582912 | tf_op jit(solution)/shard_map/all_to_all | solution.py:50
  178.3 5.3 fusion.41
  183.6 0.0 all-reduce.5.cloned.1.call-update
  183.6 0.0 reduce-scatter.2.cloned.1.call-start
  183.7 126.5 %all-reduce.5.cloned.1.call-done = f32[4096,384]{1,0:T(8,128)} async-done(((f32[4096,384]{1,0:T(8,128)}), f32[4096,384]{1,0:T(8,128)}) %all-reduce.5.cloned.1.call-update) | async-done | bytes 6291472 | tf_op jit(solution)/shard_map/psum | solution.py:55
  310.1 11.8 %fusion.8 = f32[4096,768]{1,0:T(8,128)} fusion(bf16[384,768]{1,0:T(8,128)(2,1)S(1)} %copy-done, f32[4096,384]{1,0:T(8,128)} %all-reduce.5.cloned.1.call-done), kind=kOutput, calls=%fused_computation.9 | convolution fusion | flops 2430074880 | bytes 19464192 | tf_op jit(solution)/shard_map/dot_general | solution.py:58
  321.9 0.0 reduce-scatter.2.cloned.1.call-update
  322.0 0.3 reduce-window.9
  322.3 0.1 slice.40
  323.0 0.1 slice_reduce_fusion
  323.1 0.1 multiply_bitcast_fusion
  323.2 0.6 select_reduce_fusion
  325.1 0.7 iota_compare_fusion.1
  325.8 1.3 compare_and_fusion
  327.1 167.4 %reduce-scatter.2.cloned.1.call-done = f32[128,768]{1,0:T(8,128)} async-done(((f32[4096,768]{1,0:T(8,128)}), f32[128,768]{1,0:T(8,128)}) %reduce-scatter.2.cloned.1.call-update) | async-done | bytes 393232 | tf_op jit(solution)/shard_map/reduce_scatter | solution.py:57
  494.5 1.3 convert_reduce_fusion
  495.8 0.0 copy-start.2
  495.8 10.5 %all-reduce.1 = (f32[128,1]{0,1:T(1,128)S(1)}, f32[128,1]{0,1:T(1,128)S(1)}) all-reduce(f32[128,1]{0,1:T(1,128)S(1)} %bitcast.44, f32[128,1]{0,1:T(1,128)S(1)} %bitcast.43), channel_id=1, replica_groups=mesh['cfg'=2,'wide'=32,'narrow'=4] {'narrow'}, use_global_device_ids=true, to_apply=%region_14.15 | all-reduce | flops 256 | bytes 2048 | tf_op jit(solution)/shard_map/psum | solution.py:21
  506.3 0.3 convolution_multiply_fusion
  506.6 31.1 %psum.47 = f32[128,64]{0,1:T(8,128)S(1)} all-reduce(f32[128,64]{0,1:T(8,128)S(1)} %convolution_multiply_fusion), channel_id=1, replica_groups=mesh['cfg'=2,'wide'=32,'narrow'=4] {'cfg','narrow'}, use_global_device_ids=true, to_apply=%region_15.16 | all-reduce | flops 8192 | bytes 65536 | tf_op jit(solution)/shard_map/psum | solution.py:68
  537.7 0.6 subtract_select_fusion
  (14 shorter events, 0.1 us)
Async XLA Ops:
  7.2 303.0 %copy-start = (bf16[384,768]{1,0:T(8,128)(2,1)S(1)}, bf16[384,768]{1,0:T(8,128)(2,1)}, u32[]{:S(2)}) copy-start(bf16[384,768]{1,0:T(8,128)(2,1)} %param.12) | copy-start | bytes 1769476
  7.2 302.9 %all-reduce.5.cloned.1.call-start = ((), (), s32[]{:S(2)}) async-start(), calls=%async_computation.2 | async-start | bytes 12582912 | tf_op jit(solution)/shard_map/psum | solution.py:55
  25.7 152.6 %copy-start.4 = (bf16[768,384]{1,0:T(8,128)(2,1)S(1)}, bf16[768,384]{1,0:T(8,128)(2,1)}, u32[]{:S(2)}) copy-start(bf16[768,384]{1,0:T(8,128)(2,1)} %param.11) | copy-start | bytes 1769476
  183.6 310.9 %reduce-scatter.2.cloned.1.call-start = ((), (), s32[]{:S(2)}) async-start(), calls=%async_computation.3 | async-start | bytes 12976128 | tf_op jit(solution)/shard_map/reduce_scatter | solution.py:57
  321.9 172.6 %copy-start.1 = (bf16[1,128,768]{2,1,0:T(8,128)(2,1)S(1)}, bf16[1,128,768]{2,1,0:T(8,128)(2,1)}, u32[]{:S(2)}) copy-start(bf16[1,128,768]{2,1,0:T(8,128)(2,1)} %param.8) | copy-start | bytes 589828
  321.9 184.4 %copy-start.5 = (bf16[768,64]{0,1:T(8,128)(2,1)S(1)}, bf16[768,64]{0,1:T(8,128)(2,1)}, u32[]{:S(2)}) copy-start(bf16[768,64]{0,1:T(8,128)(2,1)} %param.13) | copy-start | bytes 294916
  321.9 215.8 %copy-start.3 = (f32[128,64]{0,1:T(8,128)S(1)}, f32[128,64]{0,1:T(8,128)}, u32[]{:S(2)}) copy-start(f32[128,64]{0,1:T(8,128)} %param.14) | copy-start | bytes 98308
  495.8 42.6 %copy-start.2 = (bf16[128,768]{1,0:T(8,128)(2,1)}, bf16[128,768]{1,0:T(8,128)(2,1)S(1)}, u32[]{:S(2)}) copy-start(bf16[128,768]{1,0:T(8,128)(2,1)S(1)} %get-tuple-element.18) | copy-start | bytes 589828
Sparse Core Ops, SparseCore 0:
  183.7 126.3 all-reduce.4
  322.1 172.3 reduce-scatter.1
